TPU v7x, 256 devices: a whole 4x4x8 slice. The times are simulated.
256 devices in a mesh: wide: 32 (over y, x, core), narrow: 8 (over z).
Axes of the slice: x: 4, y: 4, z: 8, core: 2. Of those that a mesh axis runs over, the one named last changes fastest.
Arguments:
- covariates: bfloat16 [524288, 128], P(('wide', 'narrow')), may hold values from -6 to 6
- level_codes: int32 [524288], P(('wide', 'narrow')), may hold values from 0 to 3
- sign_bits: int32 [524288], P(('wide', 'narrow')), may hold values from 0 to 1
- sample_rows: int32 [1024], P(('wide', 'narrow')), may hold values from 0 to 2047, as said below
- effects: float32 [512], replicated, may hold values from -6 to 6
- noise: float32 [524288], P(('wide', 'narrow')), may hold values from -8 to 8
Outputs:
- coefficients: float32 [512], replicated
- residual: float32 [524288], P(('wide', 'narrow'))
- factor: float32 [512, 512], replicated
Inputs may be any that keep to these rules, and one draw needn't show every extreme that they name: `sample_rows`: a local row offset on the device that owns the entry.
All inputs are finite; a program needn't handle non-finite values.
Results may differ from a plain program's by a relative error of at most 0.0006.
The roundings to bfloat16 on the way count: a program that leaves them out, or rounds other values in their place, can miss the bound.
Values may be sent and summed in bfloat16 or wider, within the bound.
A program may use at most 64 MiB of HBM per device.

v0:
```python
import math
import jax
import jax.numpy as jnp
from jax import lax
from jax.sharding import PartitionSpec as P

COV = 128
LEVELS = 4
HB = 256
SKETCH = 1024
ITERS = 4
half_root = math.sqrt(0.5)


def partner(value, axis, apart):
    mask = 2**apart
    pairs = [(source, source ^ mask) for source in range(lax.axis_size(axis))]
    return lax.ppermute(value, axis, pairs)


def hadamard(size):
    left = jnp.arange(size, dtype=jnp.int32)[:, None]
    right = jnp.arange(size, dtype=jnp.int32)[None, :]
    common = jnp.bitwise_and(left, right)
    parity = jnp.zeros((size, size), jnp.int32)
    for place in range(size.bit_length()):
        parity = parity + jnp.bitwise_and(jnp.right_shift(common, place), 1)
    return (1 - 2 * (parity % 2)).astype(jnp.bfloat16)


def tri_solve(lower, vector, transpose):
    return lax.linalg.triangular_solve(
        lower, vector[:, None], left_side=True, lower=True, transpose_a=transpose
    )[:, 0]


def combine_pair(own, theirs, upper):
    own_wide = own.astype(jnp.float32)
    their_wide = theirs.astype(jnp.float32)
    low = jnp.where(upper, their_wide, own_wide)
    high = jnp.where(upper, own_wide, their_wide)
    return (jnp.where(upper, low - high, low + high) * half_root).astype(jnp.bfloat16)


def body(covariates, level_codes, sign_bits, sample_rows, effects, noise):
    rows_dev = covariates.shape[0]
    cols = LEVELS * COV
    onehot = (level_codes[:, None] == jnp.arange(LEVELS, dtype=jnp.int32)[None, :]).astype(
        jnp.float32
    )
    flipped = covariates * (1 - 2 * sign_bits).astype(jnp.bfloat16)[:, None]
    design = (onehot.astype(jnp.bfloat16)[:, :, None] * flipped[:, None, :]).reshape(
        rows_dev // HB, HB, cols
    )
    local = jnp.einsum("ij,gjc->gic", hadamard(HB), design, preferred_element_type=jnp.float32)
    local = (local * (1.0 / math.sqrt(HB))).astype(jnp.bfloat16).reshape(rows_dev, cols)
    wide_index = lax.axis_index("wide")
    mixed = local
    for place in range(3):
        upper = jnp.bitwise_and(jnp.right_shift(wide_index, place), 1) == 1
        theirs = partner(mixed, "wide", place)
        mixed = combine_pair(mixed, theirs, upper)
    sketch = mixed[sample_rows]
    gram = lax.psum(
        jnp.dot(sketch.T, sketch, preferred_element_type=jnp.float32), ("wide", "narrow")
    )
    lower = jnp.linalg.cholesky(gram)
    factor = lower.T * math.sqrt(LEVELS / SKETCH)
    wide_cov = covariates.astype(jnp.float32)

    def apply_design(vector):
        values = jnp.dot(wide_cov, vector.reshape(LEVELS, COV).T, precision=lax.Precision.HIGHEST)
        return jnp.sum(values * onehot, axis=1)

    def adjoint(vector):
        return jnp.dot(
            (onehot * vector[:, None]).T, wide_cov, precision=lax.Precision.HIGHEST
        ).reshape(cols)

    resid = apply_design(effects) + noise
    gradient_now = lax.psum(adjoint(resid), ("wide", "narrow"))
    steer = tri_solve(lower, gradient_now, False)
    direction = steer
    gamma = jnp.sum(steer * steer)
    solved = jnp.zeros((cols,), jnp.float32)
    for step in range(ITERS):
        image = apply_design(tri_solve(lower, direction, True))
        alpha = gamma / lax.psum(jnp.sum(image * image), ("wide", "narrow"))
        solved = solved + alpha * direction
        resid = resid - alpha * image
        gradient_now = lax.psum(adjoint(resid), ("wide", "narrow"))
        steer = tri_solve(lower, gradient_now, False)
        gamma_new = jnp.sum(steer * steer)
        direction = steer + gamma_new / gamma * direction
        gamma = gamma_new
    return (tri_solve(lower, solved, True), resid, factor)


def solution(mesh):
    return jax.shard_map(
        body,
        mesh=mesh,
        in_specs=(
            P(("wide", "narrow"), None),
            P(("wide", "narrow")),
            P(("wide", "narrow")),
            P(("wide", "narrow")),
            P(),
            P(("wide", "narrow")),
        ),
        out_specs=(P(), P(("wide", "narrow")), P()),
        check_vma=False,
    )
```

profile of v0, /device:TPU:1, one launch (start us, length us, event | category | flops | bytes accessed | tf_op | source)
XLA Modules:
  0.0 1097.9 jit_solution(14000195256907005070)
XLA Ops:
  10.4 7.2 broadcast_multiply_fusion
  17.6 2.2 mul.220
  19.8 2.6 multiply_convert_fusion.3
  22.4 3.3 collective-permute-start
  25.7 3.9 collective-permute-done
  29.6 4.1 multiply_convert_fusion.2
  33.8 47.2 %collective-permute-done.1 = bf16[2048,512]{1,0:T(8,128)(2,1)} collective-permute-done((bf16[2048,512]{1,0:T(8,128)(2,1)}, bf16[2048,512]{1,0:T(8,128)(2,1)}, u32[]{:S(2)}, u32[]{:S(2)}) %collective-permute-start.1) | collective-permute-done | bytes 2097184 | tf_op jit(solution)/shard_map/ppermute | solution.py:18
  80.9 3.4 multiply_convert_fusion.1
  85.4 46.5 %collective-permute-done.2 = bf16[2048,512]{1,0:T(8,128)(2,1)} collective-permute-done((bf16[2048,512]{1,0:T(8,128)(2,1)S(1)}, bf16[2048,512]{1,0:T(8,128)(2,1)}, u32[]{:S(2)}, u32[]{:S(2)}) %collective-permute-start.2) | collective-permute-done | bytes 2097184 | tf_op jit(solution)/shard_map/ppermute | solution.py:18
  131.9 4.1 multiply_convert_fusion
  136.0 2.5 gather_fusion
  140.7 79.7 %psum.64 = f32[512,1]{0,1:T(1,128)S(1)} all-reduce(f32[512,1]{0,1:T(1,128)S(1)} %bitcast.533), channel_id=1, replica_groups=mesh['wide'=32,'narrow'=8] {'wide','narrow'}, use_global_device_ids=true, to_apply=%region_10.11 | all-reduce | flops 512 | bytes 4096 | tf_op jit(solution)/shard_map/psum | solution.py:81
  220.5 176.9 %all-reduce.3.cloned.1.call-done = f32[512,512]{0,1:T(8,128)} async-done(((f32[512,512]{0,1:T(8,128)}), f32[512,512]{0,1:T(8,128)}) %all-reduce.3.cloned.1.call-update) | async-done | bytes 1048592 | tf_op jit(solution)/shard_map/psum | solution.py:64
  397.4 1.6 copy.11
  401.1 11.7 %cholesky.104 = f32[128,128]{1,0:T(8,128)S(1)} custom-call(f32[128,128]{1,0:T(8,128)S(1)} %cholesky.266), custom_call_target="Cholesky" | custom-call | tf_op jit(solution)/shard_map/jit(cholesky)/cholesky | solution.py:67
  412.8 9.8 custom-call.33
  425.3 11.7 %cholesky.217 = f32[128,128]{1,0:T(8,128)S(1)} custom-call(f32[128,128]{1,0:T(8,128)S(1)} %cholesky.270), custom_call_target="Cholesky" | custom-call | tf_op jit(solution)/shard_map/jit(cholesky)/cholesky | solution.py:67
  437.1 10.0 custom-call.34
  448.6 11.7 %cholesky.238 = f32[128,128]{1,0:T(8,128)S(1)} custom-call(f32[128,128]{1,0:T(8,128)S(1)} %cholesky.275), custom_call_target="Cholesky" | custom-call | tf_op jit(solution)/shard_map/jit(cholesky)/cholesky | solution.py:67
  461.1 9.8 custom-call.35
  472.4 11.7 %cholesky.255 = f32[128,128]{1,0:T(8,128)S(1)} custom-call(f32[128,128]{1,0:T(8,128)S(1)} %convolution_subtract_fusion.2), custom_call_target="Cholesky" | custom-call | tf_op jit(solution)/shard_map/jit(cholesky)/cholesky | solution.py:67
  487.9 1.5 multiply_bitcast_fusion
  489.5 8.5 while.18
  490.1 1.4 bitcast_dynamic-update-slice_fusion.2
  497.9 39.3 %custom-call.51 = f32[4,128,128]{1,2,0:T(8,128)S(1)} custom-call(f32[4,128,128]{2,1,0:T(8,128)S(1)} %get-tuple-element.71), custom_call_target="InvertDiagBlocksLowerTriangular" | custom-call | tf_op jit(solution)/shard_map/triangular_solve/custom-call.8 | solution.py:32
  542.0 77.5 %psum.65 = f32[]{:T(128)} all-reduce(f32[]{:T(128)} %multiply_reduce_fusion.3), channel_id=1, replica_groups=mesh['wide'=32,'narrow'=8] {'wide','narrow'}, use_global_device_ids=true, to_apply=%region_14.17 | all-reduce | flops 1 | bytes 8 | tf_op jit(solution)/shard_map/psum | solution.py:88
  621.2 73.2 %psum.66 = f32[512,1]{0,1:T(1,128)S(1)} all-reduce(f32[512,1]{0,1:T(1,128)S(1)} %bitcast.534), channel_id=1, replica_groups=mesh['wide'=32,'narrow'=8] {'wide','narrow'}, use_global_device_ids=true, to_apply=%region_15.18 | all-reduce | flops 512 | bytes 4096 | tf_op jit(solution)/shard_map/psum | solution.py:91
  700.4 74.2 %psum.67 = f32[]{:T(128)} all-reduce(f32[]{:T(128)} %multiply_reduce_fusion.2), channel_id=1, replica_groups=mesh['wide'=32,'narrow'=8] {'wide','narrow'}, use_global_device_ids=true, to_apply=%region_19.22 | all-reduce | flops 1 | bytes 8 | tf_op jit(solution)/shard_map/psum | solution.py:88
  776.3 73.4 %psum.68 = f32[512,1]{0,1:T(1,128)S(1)} all-reduce(f32[512,1]{0,1:T(1,128)S(1)} %bitcast.535), channel_id=1, replica_groups=mesh['wide'=32,'narrow'=8] {'wide','narrow'}, use_global_device_ids=true, to_apply=%region_20.23 | all-reduce | flops 512 | bytes 4096 | tf_op jit(solution)/shard_map/psum | solution.py:91
  855.8 74.2 %psum.69 = f32[]{:T(128)} all-reduce(f32[]{:T(128)} %multiply_reduce_fusion.1), channel_id=1, replica_groups=mesh['wide'=32,'narrow'=8] {'wide','narrow'}, use_global_device_ids=true, to_apply=%region_24.27 | all-reduce | flops 1 | bytes 8 | tf_op jit(solution)/shard_map/psum | solution.py:88
  931.7 73.6 %psum.70 = f32[512,1]{0,1:T(1,128)S(1)} all-reduce(f32[512,1]{0,1:T(1,128)S(1)} %bitcast.536), channel_id=1, replica_groups=mesh['wide'=32,'narrow'=8] {'wide','narrow'}, use_global_device_ids=true, to_apply=%region_25.28 | all-reduce | flops 512 | bytes 4096 | tf_op jit(solution)/shard_map/psum | solution.py:91
  1011.3 74.1 %psum.71 = f32[]{:T(128)} all-reduce(f32[]{:T(128)} %multiply_reduce_fusion), channel_id=1, replica_groups=mesh['wide'=32,'narrow'=8] {'wide','narrow'}, use_global_device_ids=true, to_apply=%region_29.32 | all-reduce | flops 1 | bytes 8 | tf_op jit(solution)/shard_map/psum | solution.py:88
  (152 shorter events, 47.0 us)
Async XLA Ops:
  7.2 132.7 %copy-start = (f32[512]{0:T(512)S(1)}, f32[512]{0:T(512)}, u32[]{:S(2)}) copy-start(f32[512]{0:T(512)} %param.14) | copy-start | bytes 6148
  7.2 390.2 %all-reduce.3.cloned.1.call-start = ((), (), s32[]{:S(2)}) async-start(), calls=%async_computation | async-start | bytes 2097152 | tf_op jit(solution)/shard_map/psum | solution.py:64
  22.4 7.2 collective-permute-start
  33.8 47.2 %collective-permute-start.1 = (bf16[2048,512]{1,0:T(8,128)(2,1)}, bf16[2048,512]{1,0:T(8,128)(2,1)}, u32[]{:S(2)}, u32[]{:S(2)}) collective-permute-start(bf16[2048,512]{1,0:T(8,128)(2,1)} %multiply_convert_fusion.2), channel_id=1, source_target_pairs={{0,16},{8,24},{16,0},{24,8},{32,48},{40,56},{48,32},{56,40},{64,80... | collective-permute-start | bytes 6291464 | tf_op jit(solution)/shard_map/ppermute | solution.py:18
  33.8 51.7 %copy-start.6 = (s32[4]{0:T(128)S(1)}, s32[4]{0:T(128)}, u32[]{:S(2)}) copy-start(s32[4]{0:T(128)} %param.13) | copy-start | bytes 52
  84.3 47.6 %collective-permute-start.2 = (bf16[2048,512]{1,0:T(8,128)(2,1)S(1)}, bf16[2048,512]{1,0:T(8,128)(2,1)}, u32[]{:S(2)}, u32[]{:S(2)}) collective-permute-start(bf16[2048,512]{1,0:T(8,128)(2,1)S(1)} %multiply_convert_fusion.1), channel_id=1, source_target_pairs={{0,32},{8,40},{16,48},{24,56},{32,0},{40,8},{48,16},{56,24},{64,96... | collective-permute-start | bytes 6291464 | tf_op jit(solution)/shard_map/ppermute | solution.py:18
  136.0 3.9 copy-start.1
  136.0 3.9 copy-start.4
  136.0 4.4 copy-start.5
  397.4 1.7 copy-start.2
  850.3 237.1 %copy-start.3 = (f32[512,512]{0,1:T(8,128)S(1)}, f32[512,512]{0,1:T(8,128)}, u32[]{:S(2)}) copy-start(f32[512,512]{0,1:T(8,128)} %get-tuple-element.93) | copy-start | bytes 3145732
Sparse Core Ops, SparseCore 0:
  140.0 257.3 all-reduce.2
where the time goes:
time: 1110 us; the launch traced here: 1100 us
  blocking collectives  600 us (54%)
  waiting for transfers between devices  275 us (25%)
  other arithmetic  148 us (13%)
  between operations  26.6 us (2%)
  matrix products  26.4 us (2%)
  local copies, waits for them, and re-layouts  17.4 us (2%)
    psum x4, blocking collectives, body(): alpha = gamma / lax.psum(jnp.sum(image * image), ('wide', 'narrow'))  300 us
    psum x4, blocking collectives, body(): gradient_now = lax.psum(adjoint(resid), ('wide', 'narrow'))  300 us
    psum x1, waiting for transfers between devices, body(): lax.psum(jnp.dot(sketch.T, sketch, preferred_element_type=jnp.float32), (...  177 us
    ppermute x3, waiting for transfers between devices, partner(): return lax.ppermute(value, axis, pairs)  97.6 us
    another operation x14, other arithmetic, body(): lower = jnp.linalg.cholesky(gram)  78.6 us
    another operation x8, other arithmetic, tri_solve(): lax.linalg.triangular_solve(lower, vector[:, None], left_side=True, lower...  40 us
  transfers between devices with their start and end apart: 4, of which 4 were waited for; matrix products, arithmetic and copies ran while one was open for 0% of the time, Pallas kernels for 0%

commit v1 on v0

--- a/solution.py
+++ b/solution.py
@@ -78,7 +78,9 @@
         ).reshape(cols)
 
     resid = apply_design(effects) + noise
-    gradient_now = lax.psum(adjoint(resid), ("wide", "narrow"))
+    block = adjoint(resid)
+    parts = lax.all_gather(block, ("wide", "narrow"), axis=0, tiled=False)
+    gradient_now = parts.sum(axis=0)
     steer = tri_solve(lower, gradient_now, False)
     direction = steer
     gamma = jnp.sum(steer * steer)

time: 1110 us -> 1110 us (level)
    psum x4 -> x3, blocking collectives: 300 us -> 220 us  [body(): gradient_now = lax.psum(adjoint(resid), ('wide', 'narrow'))]
    all_gather x0 -> x1, blocking collectives: none -> 72.1 us  [body(): parts = lax.all_gather(block, ('wide', 'narrow'), axis=0, tiled=False)]
where the time goes in v1:
time: 1110 us; the launch traced here: 1100 us
  blocking collectives  592 us (53%)
  waiting for transfers between devices  282 us (25%)
  other arithmetic  149 us (13%)
  between operations  26.5 us (2%)
  matrix products  26.4 us (2%)
  local copies, waits for them, and re-layouts  17.4 us (2%)
    psum x4, blocking collectives, body(): alpha = gamma / lax.psum(jnp.sum(image * image), ('wide', 'narrow'))  300 us
    psum x3, blocking collectives, body(): gradient_now = lax.psum(adjoint(resid), ('wide', 'narrow'))  220 us
    psum x1, waiting for transfers between devices, body(): lax.psum(jnp.dot(sketch.T, sketch, preferred_element_type=jnp.float32), (...  185 us
    ppermute x3, waiting for transfers between devices, partner(): return lax.ppermute(value, axis, pairs)  97 us
    another operation x14, other arithmetic, body(): lower = jnp.linalg.cholesky(gram)  79 us
    all_gather x1, blocking collectives, body(): parts = lax.all_gather(block, ('wide', 'narrow'), axis=0, tiled=False)  72.1 us
    another operation x8, other arithmetic, tri_solve(): lax.linalg.triangular_solve(lower, vector[:, None], left_side=True, lower...  40 us
  transfers between devices with their start and end apart: 4, of which 4 were waited for; matrix products, arithmetic and copies ran while one was open for 0% of the time, Pallas kernels for 0%

profile of v1, /device:TPU:1, one launch (start us, length us, event | category | flops | bytes accessed | tf_op | source)
XLA Modules:
  0.0 1097.8 jit_solution(13936273339487340898)
XLA Ops:
  10.4 7.2 broadcast_multiply_fusion
  17.6 2.2 mul.220
  19.8 2.6 multiply_convert_fusion.3
  22.4 3.3 collective-permute-start
  25.7 3.9 collective-permute-done
  29.6 4.1 multiply_convert_fusion.2
  33.8 47.1 %collective-permute-done.1 = bf16[2048,512]{1,0:T(8,128)(2,1)} collective-permute-done((bf16[2048,512]{1,0:T(8,128)(2,1)}, bf16[2048,512]{1,0:T(8,128)(2,1)}, u32[]{:S(2)}, u32[]{:S(2)}) %collective-permute-start.1) | collective-permute-done | bytes 2097184 | tf_op jit(solution)/shard_map/ppermute | solution.py:18
  80.9 3.4 multiply_convert_fusion.1
  86.0 45.9 %collective-permute-done.2 = bf16[2048,512]{1,0:T(8,128)(2,1)} collective-permute-done((bf16[2048,512]{1,0:T(8,128)(2,1)S(1)}, bf16[2048,512]{1,0:T(8,128)(2,1)}, u32[]{:S(2)}, u32[]{:S(2)}) %collective-permute-start.2) | collective-permute-done | bytes 2097184 | tf_op jit(solution)/shard_map/ppermute | solution.py:18
  131.9 4.1 multiply_convert_fusion
  136.0 2.4 gather_fusion
  140.1 72.1 %all-gather = f32[256,1,512]{2,1,0:T(1,128)S(1)} all-gather(f32[1,1,512]{2,1,0:T(1,128)S(1)} %bitcast.534), channel_id=1, replica_groups=mesh['wide'=32,'narrow'=8] {'wide','narrow'}, dimensions={0}, use_global_device_ids=true | all-gather | bytes 526336 | tf_op jit(solution)/shard_map/all_gather | solution.py:82
  212.5 184.9 %all-reduce.3.cloned.1.call-done = f32[512,512]{0,1:T(8,128)} async-done(((f32[512,512]{0,1:T(8,128)}), f32[512,512]{0,1:T(8,128)}) %all-reduce.3.cloned.1.call-update) | async-done | bytes 1048592 | tf_op jit(solution)/shard_map/psum | solution.py:64
  397.4 1.6 copy.15
  401.1 11.7 %cholesky.104 = f32[128,128]{1,0:T(8,128)S(1)} custom-call(f32[128,128]{1,0:T(8,128)S(1)} %cholesky.266), custom_call_target="Cholesky" | custom-call | tf_op jit(solution)/shard_map/jit(cholesky)/cholesky | solution.py:67
  413.0 9.8 custom-call.33
  425.3 11.7 %cholesky.217 = f32[128,128]{1,0:T(8,128)S(1)} custom-call(f32[128,128]{1,0:T(8,128)S(1)} %cholesky.270), custom_call_target="Cholesky" | custom-call | tf_op jit(solution)/shard_map/jit(cholesky)/cholesky | solution.py:67
  437.1 10.0 custom-call.34
  448.6 11.7 %cholesky.238 = f32[128,128]{1,0:T(8,128)S(1)} custom-call(f32[128,128]{1,0:T(8,128)S(1)} %cholesky.275), custom_call_target="Cholesky" | custom-call | tf_op jit(solution)/shard_map/jit(cholesky)/cholesky | solution.py:67
  461.1 9.8 custom-call.35
  472.4 12.1 %cholesky.255 = f32[128,128]{1,0:T(8,128)S(1)} custom-call(f32[128,128]{1,0:T(8,128)S(1)} %convolution_subtract_fusion.2), custom_call_target="Cholesky" | custom-call | tf_op jit(solution)/shard_map/jit(cholesky)/cholesky | solution.py:67
  489.5 8.5 while.18
  490.1 1.4 bitcast_dynamic-update-slice_fusion.2
  492.2 1.4 bitcast_dynamic-update-slice_fusion.2
  497.9 39.3 %custom-call.51 = f32[4,128,128]{1,2,0:T(8,128)S(1)} custom-call(f32[4,128,128]{2,1,0:T(8,128)S(1)} %get-tuple-element.71), custom_call_target="InvertDiagBlocksLowerTriangular" | custom-call | tf_op jit(solution)/shard_map/triangular_solve/custom-call.8 | solution.py:32
  542.0 77.5 %psum.57 = f32[]{:T(128)} all-reduce(f32[]{:T(128)} %multiply_reduce_fusion.3), channel_id=1, replica_groups=mesh['wide'=32,'narrow'=8] {'wide','narrow'}, use_global_device_ids=true, to_apply=%region_14.17 | all-reduce | flops 1 | bytes 8 | tf_op jit(solution)/shard_map/psum | solution.py:90
  621.1 73.2 %psum.58 = f32[512,1]{0,1:T(1,128)S(1)} all-reduce(f32[512,1]{0,1:T(1,128)S(1)} %bitcast.539), channel_id=1, replica_groups=mesh['wide'=32,'narrow'=8] {'wide','narrow'}, use_global_device_ids=true, to_apply=%region_15.18 | all-reduce | flops 512 | bytes 4096 | tf_op jit(solution)/shard_map/psum | solution.py:93
  700.4 74.2 %psum.59 = f32[]{:T(128)} all-reduce(f32[]{:T(128)} %multiply_reduce_fusion.2), channel_id=1, replica_groups=mesh['wide'=32,'narrow'=8] {'wide','narrow'}, use_global_device_ids=true, to_apply=%region_19.22 | all-reduce | flops 1 | bytes 8 | tf_op jit(solution)/shard_map/psum | solution.py:90
  776.3 73.4 %psum.60 = f32[512,1]{0,1:T(1,128)S(1)} all-reduce(f32[512,1]{0,1:T(1,128)S(1)} %bitcast.540), channel_id=1, replica_groups=mesh['wide'=32,'narrow'=8] {'wide','narrow'}, use_global_device_ids=true, to_apply=%region_20.23 | all-reduce | flops 512 | bytes 4096 | tf_op jit(solution)/shard_map/psum | solution.py:93
  855.8 74.4 %psum.61 = f32[]{:T(128)} all-reduce(f32[]{:T(128)} %multiply_reduce_fusion.1), channel_id=1, replica_groups=mesh['wide'=32,'narrow'=8] {'wide','narrow'}, use_global_device_ids=true, to_apply=%region_24.27 | all-reduce | flops 1 | bytes 8 | tf_op jit(solution)/shard_map/psum | solution.py:90
  931.9 73.4 %psum.62 = f32[512,1]{0,1:T(1,128)S(1)} all-reduce(f32[512,1]{0,1:T(1,128)S(1)} %bitcast.541), channel_id=1, replica_groups=mesh['wide'=32,'narrow'=8] {'wide','narrow'}, use_global_device_ids=true, to_apply=%region_25.28 | all-reduce | flops 512 | bytes 4096 | tf_op jit(solution)/shard_map/psum | solution.py:93
  1011.3 74.1 %psum.63 = f32[]{:T(128)} all-reduce(f32[]{:T(128)} %multiply_reduce_fusion), channel_id=1, replica_groups=mesh['wide'=32,'narrow'=8] {'wide','narrow'}, use_global_device_ids=true, to_apply=%region_29.32 | all-reduce | flops 1 | bytes 8 | tf_op jit(solution)/shard_map/psum | solution.py:90
  (153 shorter events, 47.0 us)
Async XLA Ops:
  7.2 78.3 %copy-start = (f32[512]{0:T(512)S(1)}, f32[512]{0:T(512)}, u32[]{:S(2)}) copy-start(f32[512]{0:T(512)} %param.14) | copy-start | bytes 6148
  7.2 390.2 %all-reduce.3.cloned.1.call-start = ((), (), s32[]{:S(2)}) async-start(), calls=%async_computation | async-start | bytes 2097152 | tf_op jit(solution)/shard_map/psum | solution.py:64
  22.4 7.2 collective-permute-start
  33.8 47.2 %collective-permute-start.1 = (bf16[2048,512]{1,0:T(8,128)(2,1)}, bf16[2048,512]{1,0:T(8,128)(2,1)}, u32[]{:S(2)}, u32[]{:S(2)}) collective-permute-start(bf16[2048,512]{1,0:T(8,128)(2,1)} %multiply_convert_fusion.2), channel_id=1, source_target_pairs={{0,16},{8,24},{16,0},{24,8},{32,48},{40,56},{48,32},{56,40},{64,80... | collective-permute-start | bytes 6291464 | tf_op jit(solution)/shard_map/ppermute | solution.py:18
  33.8 51.7 %copy-start.1 = (bf16[2048,128]{1,0:T(8,128)(2,1)S(1)}, bf16[2048,128]{1,0:T(8,128)(2,1)}, u32[]{:S(2)}) copy-start(bf16[2048,128]{1,0:T(8,128)(2,1)} %param.10) | copy-start | bytes 1572868
  33.8 51.7 %copy-start.4 = (s32[2048]{0:T(1024)S(1)}, s32[2048]{0:T(1024)}, u32[]{:S(2)}) copy-start(s32[2048]{0:T(1024)} %param.11) | copy-start | bytes 24580
  33.8 52.2 %copy-start.5 = (f32[2048]{0:T(1024)S(1)}, f32[2048]{0:T(1024)}, u32[]{:S(2)}) copy-start(f32[2048]{0:T(1024)} %param.15) | copy-start | bytes 24580
  33.8 52.2 %copy-start.6 = (s32[4]{0:T(128)S(1)}, s32[4]{0:T(128)}, u32[]{:S(2)}) copy-start(s32[4]{0:T(128)} %param.13) | copy-start | bytes 52
  84.3 47.6 %collective-permute-start.2 = (bf16[2048,512]{1,0:T(8,128)(2,1)S(1)}, bf16[2048,512]{1,0:T(8,128)(2,1)}, u32[]{:S(2)}, u32[]{:S(2)}) collective-permute-start(bf16[2048,512]{1,0:T(8,128)(2,1)S(1)} %multiply_convert_fusion.1), channel_id=1, source_target_pairs={{0,32},{8,40},{16,48},{24,56},{32,0},{40,8},{48,16},{56,24},{64,96... | collective-permute-start | bytes 6291464 | tf_op jit(solution)/shard_map/ppermute | solution.py:18
  397.4 1.7 copy-start.2
  853.7 235.8 %copy-start.3 = (f32[512,512]{0,1:T(8,128)S(1)}, f32[512,512]{0,1:T(8,128)}, u32[]{:S(2)}) copy-start(f32[512,512]{0,1:T(8,128)} %get-tuple-element.96) | copy-start | bytes 3145732
Sparse Core Ops, SparseCore 0:
  139.9 257.4 all-reduce.2
